TPU v7x, 32 devices: a whole 2x2x4 slice. The times are simulated.
32 devices in a mesh: seq: 16 (over z, x, core), head: 2 (over y).
Axes of the slice: x: 2, y: 2, z: 4, core: 2. Of those that a mesh axis runs over, the one named last changes fastest.
Arguments:
- queries: bfloat16 [4096, 4096], P(('seq', 'head')), may hold values from -130 to 130
- keys: bfloat16 [4096, 1024], P(('seq', 'head')), may hold values from -5 to 5
- values: bfloat16 [4096, 1024], P(('seq', 'head')), may hold values from -6 to 6
- vertical: int32 [8, 128], P('head'), may hold values from 0 to 4095, as said below
- slash: int32 [8, 64, 40], P('head'), may hold values from -1 to 59, as said below
Outputs:
- attended: bfloat16 [4096, 4096], P(('seq', 'head'))
Inputs may be any that keep to these rules, and one draw needn't show every extreme that they name: `vertical`: for each KV head the 128 entries are distinct token positions; the 256 tokens of one seq shard hold at most 15 of them, and for every head some seq shard holds exactly that many. Each KV head h has 40 distinct block offsets d[h, n], each at least 4, and some offset of every head equals 4; slash[h, b, n] = b - d[h, n] where that is not negative, else -1.
All inputs are finite; a program needn't handle non-finite values.
Results may differ from a plain program's by a relative error of at most 0.0052.
Values may be sent and summed in bfloat16 or wider, within the bound.
No kernel may reach another device: no remote copies, remote signals or barrier semaphores. Data moves between devices by JAX's collectives and lax.ppermute only.
A program may use at most 128 MiB of HBM per device.

v0:
```python
import math
import jax
import jax.numpy as jnp
from jax import lax
from jax.sharding import PartitionSpec as P

BLK = 64
NS = 40


def live_entries(lists):
    count = lists.shape[-1]
    earlier = jnp.arange(count)[:, None] > jnp.arange(count)[None, :]
    repeated = jnp.any(earlier & (lists[..., :, None] == lists[..., None, :]), axis=-1)
    return (lists >= 0) & jnp.logical_not(repeated)


def block_attention(
    query_part,
    diag_part,
    slash_part,
    slash_live,
    slash_list,
    vert_part,
    vert_where,
    block_ids,
    head_dim,
):
    scaling = 1.0 / math.sqrt(head_dim)
    width = query_part.shape[1]
    steps = query_part.shape[0]
    rows = query_part.shape[2]
    listed = slash_part.shape[1]
    positions = block_ids[:, None] * width + jnp.arange(width, dtype=jnp.int32)[None, :]
    first = (
        jnp.einsum(
            "gqrd,gkd->gqrk",
            query_part,
            diag_part[..., :head_dim],
            preferred_element_type=jnp.float32,
        )
        * scaling
    )
    causal = jnp.arange(width)[None, :] <= jnp.arange(width)[:, None]
    first = jnp.where(causal[None, :, None, :], first, -jnp.inf)
    second = (
        jnp.einsum(
            "gqrd,gnkd->gqrnk",
            query_part,
            slash_part[..., :head_dim],
            preferred_element_type=jnp.float32,
        )
        * scaling
    )
    second = jnp.where(slash_live[:, None, None, :, None], second, -jnp.inf)
    second = second.reshape(steps, width, rows, listed * width)
    third = (
        jnp.einsum(
            "gqrd,vd->gqrv", query_part, vert_part[:, :head_dim], preferred_element_type=jnp.float32
        )
        * scaling
    )
    vert_block = vert_where // width
    covered = (vert_block[None, :] == block_ids[:, None]) | jnp.any(
        slash_live[:, :, None] & (slash_list[:, :, None] == vert_block[None, None, :]), axis=1
    )
    visible = (vert_where[None, None, :] <= positions[:, :, None]) & jnp.logical_not(covered)[
        :, None, :
    ]
    third = jnp.where(visible[:, :, None, :], third, -jnp.inf)
    scores = jnp.concatenate([first, second, third], axis=-1)
    top = jnp.max(scores, axis=-1, keepdims=True)
    expo = jnp.exp(scores - top)
    total = jnp.sum(expo, axis=-1, keepdims=True)
    weights = (expo / total).astype(jnp.bfloat16)
    w_diag = weights[..., :width]
    w_slash = weights[..., width : width + listed * width].reshape(
        steps, width, rows, listed, width
    )
    w_vert = weights[..., width + listed * width :]
    out_diag = jnp.einsum(
        "gqrk,gkd->gqrd", w_diag, diag_part[..., head_dim:], preferred_element_type=jnp.float32
    )
    out_slash = jnp.einsum(
        "gqrnk,gnkd->gqrd", w_slash, slash_part[..., head_dim:], preferred_element_type=jnp.float32
    )
    out_vert = jnp.einsum(
        "gqrv,vd->gqrd", w_vert, vert_part[:, head_dim:], preferred_element_type=jnp.float32
    )
    return (out_diag + out_slash + out_vert).astype(jnp.bfloat16)


def make_step(own_rows, head_index, vert_head, vert_where, head_dim):

    def per_step(items):
        query_part, diag_part, slash_list, slash_live, sources, ident = items
        slash_part = own_rows[sources, :, head_index]
        return block_attention(
            query_part,
            diag_part,
            slash_part,
            slash_live,
            slash_list,
            vert_head,
            vert_where,
            ident,
            head_dim,
        )

    return per_step


def body(queries, keys, values, vertical, slash):
    query_rows, key_rows, value_rows = (
        lax.all_to_all(queries, "head", split_axis=1, concat_axis=0, tiled=True),
        lax.all_to_all(keys, "head", split_axis=1, concat_axis=0, tiled=True),
        lax.all_to_all(values, "head", split_axis=1, concat_axis=0, tiled=True),
    )
    shards = lax.axis_size("seq")
    seq_rank = lax.axis_index("seq")
    tok_count = key_rows.shape[0]
    local_heads = vertical.shape[0]
    head_dim = key_rows.shape[1] // local_heads
    group = query_rows.shape[1] // key_rows.shape[1]
    blocks_here = tok_count // BLK
    first_block = seq_rank * blocks_here
    paired = jnp.concatenate(
        [
            key_rows.reshape(tok_count, local_heads, head_dim),
            value_rows.reshape(tok_count, local_heads, head_dim),
        ],
        axis=2,
    )
    by_dest = slash.reshape(local_heads, shards, blocks_here * NS)
    own_ids = first_block + jnp.arange(blocks_here, dtype=jnp.int32)
    needed = jnp.any(by_dest[:, :, :, None] == own_ids[None, None, None, :], axis=2)
    needed = jnp.transpose(needed, (1, 2, 0))
    own_blocks = paired.reshape(blocks_here, BLK, local_heads, 2 * head_dim)
    outgoing = jnp.where(needed[:, :, None, :, None], own_blocks[None], jnp.zeros((), jnp.bfloat16))
    outgoing = outgoing.reshape(shards, tok_count, local_heads, 2 * head_dim)
    vert_shard = vertical // tok_count
    owned = vert_shard == seq_rank
    local_where = vertical - seq_rank * tok_count
    incoming = lax.all_to_all(outgoing, "seq", split_axis=0, concat_axis=0, tiled=True)
    token_iota = jnp.arange(tok_count)
    select = ((local_where[:, :, None] == token_iota[None, None, :]) & owned[:, :, None]).astype(
        jnp.bfloat16
    )
    partial_rows = jnp.einsum("hvt,thx->hvx", select, paired, preferred_element_type=jnp.float32)
    vert_part = lax.psum(partial_rows, "seq").astype(jnp.bfloat16)
    mine = lax.dynamic_slice_in_dim(slash, first_block, blocks_here, axis=1)
    live = live_entries(mine)
    source_block = jnp.where(live, mine, 0)
    step_blocks = math.gcd(blocks_here, 2)
    steps_count = blocks_here // step_blocks
    block_ids = (first_block + jnp.arange(blocks_here, dtype=jnp.int32)).reshape(
        steps_count, step_blocks
    )
    query_all = query_rows.reshape(steps_count, step_blocks, BLK, local_heads, group, head_dim)
    all_blocks = incoming.reshape(shards * blocks_here, BLK, local_heads, 2 * head_dim)
    results = []
    for head_index in range(local_heads):
        per_step = make_step(
            all_blocks, head_index, vert_part[head_index], vertical[head_index], head_dim
        )
        diag_all = paired[:, head_index].reshape(steps_count, step_blocks, BLK, 2 * head_dim)
        lists = mine[head_index].reshape(steps_count, step_blocks, NS)
        lives = live[head_index].reshape(steps_count, step_blocks, NS)
        sources = source_block[head_index].reshape(steps_count, step_blocks, NS)
        outputs = lax.map(
            per_step, (query_all[:, :, :, head_index], diag_all, lists, lives, sources, block_ids)
        )
        results.append(outputs)
    stacked = jnp.stack(results, axis=3).reshape(tok_count, local_heads * group * head_dim)
    return lax.all_to_all(stacked, "head", split_axis=0, concat_axis=1, tiled=True)


def solution(mesh):
    in_specs = (
        P(("seq", "head"), None),
        P(("seq", "head"), None),
        P(("seq", "head"), None),
        P("head", None),
        P("head", None, None),
    )
    out_specs = P(("seq", "head"), None)
    return jax.shard_map(body, mesh=mesh, in_specs=in_specs, out_specs=out_specs, check_vma=False)
```

profile of v0, /device:TPU:11, one launch (start us, length us, event | category | flops | bytes accessed | tf_op | source)
XLA Modules:
  0.0 733.0 jit_solution(8951616375855945567)
XLA Ops:
  14.6 4.4 all-to-all-done.2
  22.8 5.8 broadcast_select_fusion
  28.5 6.1 all-to-all-done
  34.7 8.3 %all-to-all-start.3 = ((bf16[16,256,4,256]{3,1,2,0:T(8,128)(2,1)}), bf16[16,256,4,256]{3,1,2,0:T(8,128)(2,1)}, u32[]{:S(2)}, u32[]{:S(2)}) async-start(bf16[16,256,4,256]{3,1,2,0:T(8,128)(2,1)} %broadcast_select_fusion), calls=%async_computation.3 | async-start | bytes 16777216 | tf_op jit(solution)/shard_map/all_to_all | solution.py:144
  48.8 219.5 %all-reduce.5 = bf16[4,128,256]{2,1,0:T(8,128)(2,1)S(1)} all-reduce(f32[4,128,256]{2,1,0:T(8,128)S(1)} %fusion.118), channel_id=1, replica_groups=mesh['seq'=16,'head'=2] {'seq'}, use_global_device_ids=true, to_apply=%region_2.3 | all-reduce | flops 131072 | bytes 786432 | tf_op jit(solution)/shard_map/psum | solution.py:150
  271.7 7.7 %copy.163 = bf16[16,256,4,256]{3,1,0,2:T(8,128)(2,1)} copy(bf16[16,256,4,256]{3,1,2,0:T(8,128)(2,1)} %all-to-all-done.3) | data formatting | bytes 16777216 | tf_op jit(solution)/shard_map/all_to_all | solution.py:144
  279.4 8.3 %copy.165 = bf16[64,64,4,256]{3,1,2,0:T(8,128)(2,1)} copy(bf16[64,64,4,256]{3,1,0,2:T(8,128)(2,1)} %bitcast.710) | data formatting | bytes 16777216 | tf_op jit(solution)/shard_map/while | solution.py:170
  288.5 107.5 %while.52 = (s32[]{:T(128)}, bf16[2,2,64,4,128]{4,2,3,1,0:T(8,128)(2,1)}, bf16[2,2,64,4,128]{4,3,2,1,0:T(4,128)(2,1)}, bf16[2,2,64,256]{3,2,1,0:T(8,128)(2,1)}, ...) while((s32[]{:T(128)}, ...), condition=%wide.region_9.10_spmd, body=%wide.region_3.9_spmd.sunk | while | flops 732959872 | bytes 101075352 | solution.py:170
  293.6 4.3 gather_fusion
  298.0 4.9 fusion.201
  302.9 9.2 %copy.334 = f32[2,64,4,2560]{3,1,2,0:T(8,128)} copy(f32[2,64,4,2560]{1,3,2,0:T(8,128)} %bitcast.698) | data formatting | bytes 10485760 | tf_op jit(solution)/shard_map/while/body/eval_jaxpr/reshape | solution.py:56
  312.4 7.2 concatenate.63
  319.6 3.7 fusion.205
  328.7 7.6 %reshape.1116 = bf16[2,64,4,40,64]{4,3,1,2,0:T(8,128)(2,1)} reshape(bf16[2,64,4,2560]{3,1,2,0:T(8,128)(2,1)} %slice.620) | data formatting | bytes 5242880 | tf_op jit(solution)/shard_map/while/body/eval_jaxpr/reshape | solution.py:77
  336.3 4.1 fusion.206
  347.3 4.3 gather_fusion
  351.7 4.9 fusion.201
  356.6 9.2 %copy.334 = f32[2,64,4,2560]{3,1,2,0:T(8,128)} copy(f32[2,64,4,2560]{1,3,2,0:T(8,128)} %bitcast.698) | data formatting | bytes 10485760 | tf_op jit(solution)/shard_map/while/body/eval_jaxpr/reshape | solution.py:56
  366.1 7.2 concatenate.63
  373.3 3.7 fusion.205
  382.4 7.6 %reshape.1116 = bf16[2,64,4,40,64]{4,3,1,2,0:T(8,128)(2,1)} reshape(bf16[2,64,4,2560]{3,1,2,0:T(8,128)(2,1)} %slice.620) | data formatting | bytes 5242880 | tf_op jit(solution)/shard_map/while/body/eval_jaxpr/reshape | solution.py:77
  389.9 4.1 fusion.206
  396.7 103.0 %while.53 = (s32[]{:T(128)}, bf16[2,2,64,4,128]{4,2,3,1,0:T(8,128)(2,1)}, bf16[2,2,64,4,128]{4,3,2,1,0:T(4,128)(2,1)S(1)}, bf16[2,2,64,256]{3,2,1,0:T(8,128)(2,1...) while((s32[]{:T(128)}, ...), condition=%wide.region_16.17_spmd, body=%wide.region_10.16_spmd.sunk | while | flops 732960000 | bytes 100545856 | solution.py:170
  400.7 4.3 gather_fusion.1
  405.0 4.9 fusion.213
  410.0 9.1 %copy.339 = f32[2,64,4,2560]{3,1,2,0:T(8,128)} copy(f32[2,64,4,2560]{1,3,2,0:T(8,128)} %bitcast.699) | data formatting | bytes 10485760 | tf_op jit(solution)/shard_map/while/body/eval_jaxpr/reshape | solution.py:56
  419.4 7.2 concatenate.65
  426.6 3.7 fusion.217
  435.7 7.6 %reshape.1120 = bf16[2,64,4,40,64]{4,3,1,2,0:T(8,128)(2,1)} reshape(bf16[2,64,4,2560]{3,1,2,0:T(8,128)(2,1)} %slice.629) | data formatting | bytes 5242880 | tf_op jit(solution)/shard_map/while/body/eval_jaxpr/reshape | solution.py:77
  443.2 4.1 fusion.218
  452.0 4.3 gather_fusion.1
  456.3 4.9 fusion.213
  461.2 9.1 %copy.339 = f32[2,64,4,2560]{3,1,2,0:T(8,128)} copy(f32[2,64,4,2560]{1,3,2,0:T(8,128)} %bitcast.699) | data formatting | bytes 10485760 | tf_op jit(solution)/shard_map/while/body/eval_jaxpr/reshape | solution.py:56
  470.7 7.2 concatenate.65
  477.9 3.7 fusion.217
  487.0 7.6 %reshape.1120 = bf16[2,64,4,40,64]{4,3,1,2,0:T(8,128)(2,1)} reshape(bf16[2,64,4,2560]{3,1,2,0:T(8,128)(2,1)} %slice.629) | data formatting | bytes 5242880 | tf_op jit(solution)/shard_map/while/body/eval_jaxpr/reshape | solution.py:77
  494.5 4.1 fusion.218
  500.5 107.4 %while.54 = (s32[]{:T(128)}, bf16[2,2,64,4,128]{4,2,3,1,0:T(8,128)(2,1)}, bf16[2,2,64,4,128]{4,3,2,1,0:T(4,128)(2,1)}, bf16[2,2,64,256]{3,2,1,0:T(8,128)(2,1)}, ...) while((s32[]{:T(128)}, ...), condition=%wide.region_23.24_spmd, body=%wide.region_17.23_spmd.sunk | while | flops 732960000 | bytes 101332344 | solution.py:170
  506.5 4.3 gather_fusion.2
  510.8 4.9 fusion.225
  515.7 9.2 %copy.344 = f32[2,64,4,2560]{3,1,2,0:T(8,128)} copy(f32[2,64,4,2560]{1,3,2,0:T(8,128)} %bitcast.700) | data formatting | bytes 10485760 | tf_op jit(solution)/shard_map/while/body/eval_jaxpr/reshape | solution.py:56
  525.3 7.2 concatenate.67
  541.6 7.6 %reshape.1124 = bf16[2,64,4,40,64]{4,3,1,2,0:T(8,128)(2,1)} reshape(bf16[2,64,4,2560]{3,1,2,0:T(8,128)(2,1)} %slice.638) | data formatting | bytes 5242880 | tf_op jit(solution)/shard_map/while/body/eval_jaxpr/reshape | solution.py:77
  549.1 4.2 fusion.230
  560.0 4.3 gather_fusion.2
  564.4 4.9 fusion.225
  569.3 9.2 %copy.344 = f32[2,64,4,2560]{3,1,2,0:T(8,128)} copy(f32[2,64,4,2560]{1,3,2,0:T(8,128)} %bitcast.700) | data formatting | bytes 10485760 | tf_op jit(solution)/shard_map/while/body/eval_jaxpr/reshape | solution.py:56
  578.8 7.2 concatenate.67
  595.1 7.6 %reshape.1124 = bf16[2,64,4,40,64]{4,3,1,2,0:T(8,128)(2,1)} reshape(bf16[2,64,4,2560]{3,1,2,0:T(8,128)(2,1)} %slice.638) | data formatting | bytes 5242880 | tf_op jit(solution)/shard_map/while/body/eval_jaxpr/reshape | solution.py:77
  602.7 4.2 fusion.230
  608.7 102.8 %while.55 = (s32[]{:T(128)}, bf16[2,2,64,4,128]{4,2,3,1,0:T(8,128)(2,1)}, bf16[2,2,64,4,128]{4,3,2,1,0:T(4,128)(2,1)S(1)}, bf16[2,2,64,256]{3,2,1,0:T(8,128)(2,1...) while((s32[]{:T(128)}, ...), condition=%wide.region_30.31_spmd, body=%wide.region_24.30_spmd.sunk | while | flops 732960000 | bytes 100545856 | solution.py:170
  612.4 4.3 gather_fusion.3
  616.7 4.9 fusion.237
  621.6 9.2 %copy.349 = f32[2,64,4,2560]{3,1,2,0:T(8,128)} copy(f32[2,64,4,2560]{1,3,2,0:T(8,128)} %bitcast.701) | data formatting | bytes 10485760 | tf_op jit(solution)/shard_map/while/body/eval_jaxpr/reshape | solution.py:56
  631.1 7.2 concatenate.69
  647.4 7.6 %reshape.1128 = bf16[2,64,4,40,64]{4,3,1,2,0:T(8,128)(2,1)} reshape(bf16[2,64,4,2560]{3,1,2,0:T(8,128)(2,1)} %slice.647) | data formatting | bytes 5242880 | tf_op jit(solution)/shard_map/while/body/eval_jaxpr/reshape | solution.py:77
  655.0 4.1 fusion.242
  663.7 4.3 gather_fusion.3
  668.0 4.9 fusion.237
  672.9 9.2 %copy.349 = f32[2,64,4,2560]{3,1,2,0:T(8,128)} copy(f32[2,64,4,2560]{1,3,2,0:T(8,128)} %bitcast.701) | data formatting | bytes 10485760 | tf_op jit(solution)/shard_map/while/body/eval_jaxpr/reshape | solution.py:56
  682.4 7.2 concatenate.69
  698.7 7.6 %reshape.1128 = bf16[2,64,4,40,64]{4,3,1,2,0:T(8,128)(2,1)} reshape(bf16[2,64,4,2560]{3,1,2,0:T(8,128)(2,1)} %slice.647) | data formatting | bytes 5242880 | tf_op jit(solution)/shard_map/while/body/eval_jaxpr/reshape | solution.py:77
  706.3 4.1 fusion.242
  714.4 16.4 %all_to_all.72 = bf16[2,128,2048]{2,1,0:T(8,128)(2,1)S(1)} all-to-all(bf16[2,128,2048]{2,1,0:T(8,128)(2,1)S(1)} %all_to_all.63), channel_id=1, replica_groups=mesh['seq'=16,'head'=2] {'head'}, dimensions={0} | all-to-all | bytes 2097152 | tf_op jit(solution)/shard_map/all_to_all | solution.py:175
  (276 shorter events, 141.0 us)
Async XLA Ops:
  1.7 9.4 %all-to-all-start.1 = ((bf16[128,2,512]{2,0,1:T(8,128)(2,1)}), bf16[128,2,512]{2,0,1:T(8,128)(2,1)S(1)}, u32[]{:S(2)}, u32[]{:S(2)}) async-start(bf16[128,2,512]{2,0,1:T(8,128)(2,1)} %bitcast.489), calls=%async_computation.1 | async-start | bytes 524288 | tf_op jit(solution)/shard_map/all_to_all | solution.py:116
  11.0 8.0 %all-to-all-start.2 = ((bf16[128,2,512]{2,0,1:T(8,128)(2,1)}), bf16[128,2,512]{2,0,1:T(8,128)(2,1)S(1)}, u32[]{:S(2)}, u32[]{:S(2)}) async-start(bf16[128,2,512]{2,0,1:T(8,128)(2,1)} %bitcast.488), calls=%async_computation.2 | async-start | bytes 524288 | tf_op jit(solution)/shard_map/all_to_all | solution.py:117
  19.0 15.7 %all-to-all-start = ((bf16[128,2,2048]{2,0,1:T(8,128)(2,1)}), bf16[128,2,2048]{2,0,1:T(8,128)(2,1)S(1)}, u32[]{:S(2)}, u32[]{:S(2)}) async-start(bf16[128,2,2048]{2,0,1:T(8,128)(2,1)} %bitcast.487), calls=%async_computation | async-start | bytes 2097152 | tf_op jit(solution)/shard_map/all_to_all | solution.py:115
  28.5 18.0 %copy-start.14 = (s32[4,128]{1,0:T(4,128)S(1)}, s32[4,128]{1,0:T(4,128)}, u32[]{:S(2)}) copy-start(s32[4,128]{1,0:T(4,128)} %param.16) | copy-start | bytes 6148
  34.7 237.0 %all-to-all-start.3 = ((bf16[16,256,4,256]{3,1,2,0:T(8,128)(2,1)}), bf16[16,256,4,256]{3,1,2,0:T(8,128)(2,1)}, u32[]{:S(2)}, u32[]{:S(2)}) async-start(bf16[16,256,4,256]{3,1,2,0:T(8,128)(2,1)} %broadcast_select_fusion), calls=%async_computation.3 | async-start | bytes 16777216 | tf_op jit(solution)/shard_map/all_to_all | solution.py:144
  288.5 0.7 copy-start.16
  298.0 4.9 copy-start.4
  302.9 9.2 %copy-start.11 = (bf16[2,2,64,256]{3,2,1,0:T(8,128)(2,1)S(1)}, bf16[2,2,64,256]{3,2,1,0:T(8,128)(2,1)}, u32[]{:S(2)}) copy-start(bf16[2,2,64,256]{3,2,1,0:T(8,128)(2,1)} %get-tuple-element.1995) | copy-start | bytes 393220 | tf_op jit(solution)/shard_map/while
  319.6 4.3 copy-start
  336.3 5.9 copy-start.17
  342.2 0.6 copy-start.16
  351.6 4.9 copy-start.4
  356.6 9.2 %copy-start.11 = (bf16[2,2,64,256]{3,2,1,0:T(8,128)(2,1)S(1)}, bf16[2,2,64,256]{3,2,1,0:T(8,128)(2,1)}, u32[]{:S(2)}) copy-start(bf16[2,2,64,256]{3,2,1,0:T(8,128)(2,1)} %get-tuple-element.1995) | copy-start | bytes 393220 | tf_op jit(solution)/shard_map/while
  373.3 4.3 copy-start
  389.9 6.0 copy-start.17
  405.0 4.9 copy-start.5
  426.6 4.3 copy-start.1
  456.3 4.9 copy-start.5
  477.9 4.3 copy-start.1
  500.5 108.2 %copy-start.8 = (bf16[2,2,64,4,128]{4,3,2,1,0:T(4,128)(2,1)S(1)}, bf16[2,2,64,4,128]{4,3,2,1,0:T(4,128)(2,1)}, u32[]{:S(2)}) copy-start(bf16[2,2,64,4,128]{4,3,2,1,0:T(4,128)(2,1)} %get-tuple-element.1807) | copy-start | bytes 786436
  500.5 108.2 %copy-start.9 = (bf16[256,1,256]{2,0,1:T(8,128)(2,1)S(1)}, bf16[256,1,256]{2,0,1:T(8,128)(2,1)}, u32[]{:S(2)}) copy-start(bf16[256,1,256]{2,0,1:T(8,128)(2,1)} %get-tuple-element.1294) | copy-start | bytes 393220
  500.5 108.2 %copy-start.12 = (bf16[128,256]{1,0:T(8,128)(2,1)S(1)}, bf16[128,256]{1,0:T(8,128)(2,1)}, u32[]{:S(2)}) copy-start(bf16[128,256]{1,0:T(8,128)(2,1)} %get-tuple-element.1820) | copy-start | bytes 196612
  500.5 108.2 %copy-start.15 = (s32[1,4,40]{2,1,0:T(4,128)S(1)}, s32[1,4,40]{2,1,0:T(4,128)}, u32[]{:S(2)}) copy-start(s32[1,4,40]{2,1,0:T(4,128)} %get-tuple-element.1302) | copy-start | bytes 1924
  510.8 4.9 copy-start.6
  515.7 9.2 %copy-start.10 = (bf16[2,2,64,256]{3,2,1,0:T(8,128)(2,1)S(1)}, bf16[2,2,64,256]{3,2,1,0:T(8,128)(2,1)}, u32[]{:S(2)}) copy-start(bf16[2,2,64,256]{3,2,1,0:T(8,128)(2,1)} %get-tuple-element.1893) | copy-start | bytes 393220 | tf_op jit(solution)/shard_map/while
  532.5 4.3 copy-start.2
  549.1 4.3 copy-start.13
  564.4 4.9 copy-start.6
  569.3 9.2 %copy-start.10 = (bf16[2,2,64,256]{3,2,1,0:T(8,128)(2,1)S(1)}, bf16[2,2,64,256]{3,2,1,0:T(8,128)(2,1)}, u32[]{:S(2)}) copy-start(bf16[2,2,64,256]{3,2,1,0:T(8,128)(2,1)} %get-tuple-element.1893) | copy-start | bytes 393220 | tf_op jit(solution)/shard_map/while
  586.1 4.3 copy-start.2
  602.7 4.3 copy-start.13
  616.7 4.9 copy-start.7
  638.3 4.3 copy-start.3
  668.0 4.9 copy-start.7
  689.7 4.3 copy-start.3
where the time goes:
time: 741 us; the launch traced here: 733 us
  local copies, waits for them, and re-layouts  306 us (41%)
  blocking collectives  236 us (32%)
  matrix products  90.4 us (12%)
  other arithmetic  69.6 us (9%)
  starting transfers between devices  18.8 us (3%)
  waiting for transfers between devices  10.6 us (1%)
    psum x1, blocking collectives, body(): vert_part = lax.psum(partial_rows, 'seq').astype(jnp.bfloat16)  219 us
    reshape x8, local copies, waits for them, and re-layouts, block_attention(): second = second.reshape(steps, width, rows, listed * width)  73.5 us
    reshape x8, local copies, waits for them, and re-layouts, block_attention(): weights[..., width:width + listed * width]  60.4 us
    concatenate x8, local copies, waits for them, and re-layouts, block_attention(): scores = jnp.concatenate([first, second, third], axis=-1)  57.8 us
    dot_general x8, matrix products, block_attention(): jnp.einsum('gqrd,gnkd->gqrnk', query_part, slash_part[..., :head_dim], pr...  39.2 us
    gather x8, local copies, waits for them, and re-layouts, per_step(): slash_part = own_rows[sources, :, head_index]  34.6 us
    dot_general x8, matrix products, block_attention(): jnp.einsum('gqrnk,gnkd->gqrd', w_slash, slash_part[..., head_dim:], prefe...  33.1 us
    reduce_sum x8, other arithmetic, block_attention(): total = jnp.sum(expo, axis=-1, keepdims=True)  29.5 us
  transfers between devices with their start and end apart: 4, of which 2 were waited for; matrix products, arithmetic and copies ran while one was open for 3% of the time, Pallas kernels for 0%

commit v1 on v0

--- a/solution.py
+++ b/solution.py
@@ -6,6 +6,12 @@
 
 BLK = 64
 NS = 40
+
+
+def gather_and_add(x, axis):
+    parts = lax.all_gather(x, axis, axis=0, tiled=False)
+    total = parts.sum(axis=0)
+    return total
 
 
 def live_entries(lists):
@@ -147,7 +153,7 @@
         jnp.bfloat16
     )
     partial_rows = jnp.einsum("hvt,thx->hvx", select, paired, preferred_element_type=jnp.float32)
-    vert_part = lax.psum(partial_rows, "seq").astype(jnp.bfloat16)
+    vert_part = gather_and_add(partial_rows, "seq").astype(jnp.bfloat16)
     mine = lax.dynamic_slice_in_dim(slash, first_block, blocks_here, axis=1)
     live = live_entries(mine)
     source_block = jnp.where(live, mine, 0)

time: 741 us -> 764 us (1.031)
  waiting for transfers between devices: 10.6 us -> 234 us
  blocking collectives: 236 us -> 16 us
  between operations: 0.43 us -> 13.8 us
    all_to_all x1, waiting for transfers between devices: 0.01 us -> 223 us  [body(): lax.all_to_all(outgoing, 'seq', split_axis=0, concat_axis=0, tiled=True)]
    psum x1 -> x0, blocking collectives: 219 us -> none  [body(): vert_part = lax.psum(partial_rows, 'seq').astype(jnp.bfloat16)]
  transfers between devices with their start and end apart: 4 -> 5, of which waited for: 2 -> 3; matrix products, arithmetic and copies ran while one was open for 3% -> 5% of each run, Pallas kernels for 0% -> 0%
where the time goes in v1:
time: 764 us; the launch traced here: 756 us
  local copies, waits for them, and re-layouts  305 us (40%)
  waiting for transfers between devices  234 us (31%)
  matrix products  91.1 us (12%)
  other arithmetic  74.9 us (10%)
  starting transfers between devices  18.9 us (2%)
  blocking collectives  16 us (2%)
  between operations  13.8 us (2%)
    all_to_all x1, waiting for transfers between devices, body(): lax.all_to_all(outgoing, 'seq', split_axis=0, concat_axis=0, tiled=True)  223 us
    reshape x8, local copies, waits for them, and re-layouts, block_attention(): second = second.reshape(steps, width, rows, listed * width)  73 us
    reshape x8, local copies, waits for them, and re-layouts, block_attention(): weights[..., width:width + listed * width]  60.4 us
    concatenate x8, local copies, waits for them, and re-layouts, block_attention(): scores = jnp.concatenate([first, second, third], axis=-1)  57.7 us
    dot_general x8, matrix products, block_attention(): jnp.einsum('gqrd,gnkd->gqrnk', query_part, slash_part[..., :head_dim], pr...  39.1 us
    gather x8, local copies, waits for them, and re-layouts, per_step(): slash_part = own_rows[sources, :, head_index]  34.6 us
    dot_general x8, matrix products, block_attention(): jnp.einsum('gqrnk,gnkd->gqrd', w_slash, slash_part[..., head_dim:], prefe...  33.1 us
    reduce_sum x8, other arithmetic, block_attention(): total = jnp.sum(expo, axis=-1, keepdims=True)  29.5 us
  transfers between devices with their start and end apart: 5, of which 3 were waited for; matrix products, arithmetic and copies ran while one was open for 5% of the time, Pallas kernels for 0%

profile of v1, /device:TPU:11, one launch (start us, length us, event | category | flops | bytes accessed | tf_op | source)
XLA Modules:
  0.0 755.5 jit_solution(11178071733857756373)
XLA Ops:
  22.5 4.4 all-to-all-done.2
  30.7 5.8 broadcast_select_fusion
  36.5 6.1 all-to-all-done
  42.6 8.3 %all-to-all-start.3 = ((bf16[16,256,4,256]{3,1,2,0:T(8,128)(2,1)}), bf16[16,256,4,256]{3,1,2,0:T(8,128)(2,1)}, u32[]{:S(2)}, u32[]{:S(2)}) async-start(bf16[16,256,4,256]{3,1,2,0:T(8,128)(2,1)} %broadcast_select_fusion), calls=%async_computation.3 | async-start | bytes 16777216 | tf_op jit(solution)/shard_map/all_to_all | solution.py:150
  60.5 223.4 %all-to-all-done.3 = bf16[16,256,4,256]{3,1,2,0:T(8,128)(2,1)} async-done(((bf16[16,256,4,256]{3,1,2,0:T(8,128)(2,1)}), bf16[16,256,4,256]{3,1,2,0:T(8,128)(2,1)}, u32[]{:S(2)}, u32[]{:S(2)}) %all-to-all-start.3) | async-done | bytes 8388640 | tf_op jit(solution)/shard_map/all_to_all | solution.py:150
  283.8 7.7 %copy.163 = bf16[16,256,4,256]{3,1,0,2:T(8,128)(2,1)} copy(bf16[16,256,4,256]{3,1,2,0:T(8,128)(2,1)} %all-to-all-done.3) | data formatting | bytes 16777216 | tf_op jit(solution)/shard_map/all_to_all | solution.py:150
  291.6 8.3 %copy.165 = bf16[64,64,4,256]{3,1,2,0:T(8,128)(2,1)} copy(bf16[64,64,4,256]{3,1,0,2:T(8,128)(2,1)} %bitcast.711) | data formatting | bytes 16777216 | tf_op jit(solution)/shard_map/while | solution.py:176
  299.8 4.0 reduce_sum.61
  305.3 107.0 %while.52 = (s32[]{:T(128)}, bf16[2,2,64,4,128]{4,2,3,1,0:T(8,128)(2,1)}, bf16[2,2,64,4,128]{4,3,2,1,0:T(4,128)(2,1)}, bf16[2,2,64,256]{3,2,1,0:T(8,128)(2,1)}, ...) while((s32[]{:T(128)}, ...), condition=%wide.region_9.10_spmd, body=%wide.region_3.9_spmd.sunk | while | flops 732959872 | bytes 101075352 | solution.py:176
  310.3 4.3 gather_fusion
  314.7 4.9 fusion.201
  319.5 9.1 %copy.334 = f32[2,64,4,2560]{3,1,2,0:T(8,128)} copy(f32[2,64,4,2560]{1,3,2,0:T(8,128)} %bitcast.699) | data formatting | bytes 10485760 | tf_op jit(solution)/shard_map/while/body/eval_jaxpr/reshape | solution.py:62
  329.0 7.2 concatenate.63
  336.2 3.7 fusion.205
  345.3 7.6 %reshape.1117 = bf16[2,64,4,40,64]{4,3,1,2,0:T(8,128)(2,1)} reshape(bf16[2,64,4,2560]{3,1,2,0:T(8,128)(2,1)} %slice.620) | data formatting | bytes 5242880 | tf_op jit(solution)/shard_map/while/body/eval_jaxpr/reshape | solution.py:83
  352.8 4.1 fusion.206
  363.8 4.3 gather_fusion
  368.2 4.9 fusion.201
  373.0 9.1 %copy.334 = f32[2,64,4,2560]{3,1,2,0:T(8,128)} copy(f32[2,64,4,2560]{1,3,2,0:T(8,128)} %bitcast.699) | data formatting | bytes 10485760 | tf_op jit(solution)/shard_map/while/body/eval_jaxpr/reshape | solution.py:62
  382.5 7.2 concatenate.63
  389.7 3.7 fusion.205
  398.8 7.6 %reshape.1117 = bf16[2,64,4,40,64]{4,3,1,2,0:T(8,128)(2,1)} reshape(bf16[2,64,4,2560]{3,1,2,0:T(8,128)(2,1)} %slice.620) | data formatting | bytes 5242880 | tf_op jit(solution)/shard_map/while/body/eval_jaxpr/reshape | solution.py:83
  406.3 4.1 fusion.206
  413.1 103.0 %while.53 = (s32[]{:T(128)}, bf16[2,2,64,4,128]{4,2,3,1,0:T(8,128)(2,1)}, bf16[2,2,64,4,128]{4,3,2,1,0:T(4,128)(2,1)S(1)}, bf16[2,2,64,256]{3,2,1,0:T(8,128)(2,1...) while((s32[]{:T(128)}, ...), condition=%wide.region_16.17_spmd, body=%wide.region_10.16_spmd.sunk | while | flops 732960000 | bytes 100545856 | solution.py:176
  417.1 4.3 gather_fusion.1
  421.4 4.9 fusion.213
  426.3 9.1 %copy.339 = f32[2,64,4,2560]{3,1,2,0:T(8,128)} copy(f32[2,64,4,2560]{1,3,2,0:T(8,128)} %bitcast.700) | data formatting | bytes 10485760 | tf_op jit(solution)/shard_map/while/body/eval_jaxpr/reshape | solution.py:62
  435.8 7.2 concatenate.65
  452.1 7.6 reshape.1121
  459.6 4.1 fusion.218
  468.3 4.3 gather_fusion.1
  472.6 4.9 fusion.213
  477.6 9.1 %copy.339 = f32[2,64,4,2560]{3,1,2,0:T(8,128)} copy(f32[2,64,4,2560]{1,3,2,0:T(8,128)} %bitcast.700) | data formatting | bytes 10485760 | tf_op jit(solution)/shard_map/while/body/eval_jaxpr/reshape | solution.py:62
  487.0 7.2 concatenate.65
  494.2 3.7 fusion.217
  503.3 7.6 reshape.1121
  510.9 4.1 fusion.218
  516.8 107.4 %while.54 = (s32[]{:T(128)}, bf16[2,2,64,4,128]{4,2,3,1,0:T(8,128)(2,1)}, bf16[2,2,64,4,128]{4,3,2,1,0:T(4,128)(2,1)}, bf16[2,2,64,256]{3,2,1,0:T(8,128)(2,1)}, ...) while((s32[]{:T(128)}, ...), condition=%wide.region_23.24_spmd, body=%wide.region_17.23_spmd.sunk | while | flops 732960000 | bytes 101332344 | solution.py:176
  522.9 4.3 gather_fusion.2
  527.2 4.9 fusion.225
  532.1 9.1 %copy.344 = f32[2,64,4,2560]{3,1,2,0:T(8,128)} copy(f32[2,64,4,2560]{1,3,2,0:T(8,128)} %bitcast.701) | data formatting | bytes 10485760 | tf_op jit(solution)/shard_map/while/body/eval_jaxpr/reshape | solution.py:62
  541.6 7.2 concatenate.67
  557.8 7.5 reshape.1125
  565.4 4.2 fusion.230
  576.4 4.3 gather_fusion.2
  580.7 4.9 fusion.225
  585.6 9.1 %copy.344 = f32[2,64,4,2560]{3,1,2,0:T(8,128)} copy(f32[2,64,4,2560]{1,3,2,0:T(8,128)} %bitcast.701) | data formatting | bytes 10485760 | tf_op jit(solution)/shard_map/while/body/eval_jaxpr/reshape | solution.py:62
  595.1 7.2 concatenate.67
  611.4 7.5 reshape.1125
  618.9 4.2 fusion.230
  624.9 102.6 %while.55 = (s32[]{:T(128)}, bf16[2,2,64,4,128]{4,2,3,1,0:T(8,128)(2,1)}, bf16[2,2,64,4,128]{4,3,2,1,0:T(4,128)(2,1)S(1)}, bf16[2,2,64,256]{3,2,1,0:T(8,128)(2,1...) while((s32[]{:T(128)}, ...), condition=%wide.region_30.31_spmd, body=%wide.region_24.30_spmd.sunk | while | flops 732960000 | bytes 100545856 | solution.py:176
  628.6 4.3 gather_fusion.3
  633.0 4.9 fusion.237
  637.9 9.1 %copy.349 = f32[2,64,4,2560]{3,1,2,0:T(8,128)} copy(f32[2,64,4,2560]{1,3,2,0:T(8,128)} %bitcast.702) | data formatting | bytes 10485760 | tf_op jit(solution)/shard_map/while/body/eval_jaxpr/reshape | solution.py:62
  647.3 7.2 concatenate.69
  663.6 7.5 reshape.1129
  671.1 4.1 fusion.242
  679.8 4.3 gather_fusion.3
  684.2 4.9 fusion.237
  689.1 9.1 %copy.349 = f32[2,64,4,2560]{3,1,2,0:T(8,128)} copy(f32[2,64,4,2560]{1,3,2,0:T(8,128)} %bitcast.702) | data formatting | bytes 10485760 | tf_op jit(solution)/shard_map/while/body/eval_jaxpr/reshape | solution.py:62
  698.5 7.2 concatenate.69
  714.8 7.5 reshape.1129
  722.3 4.1 fusion.242
  730.5 16.0 %all_to_all.72 = bf16[2,128,2048]{2,1,0:T(8,128)(2,1)S(1)} all-to-all(bf16[2,128,2048]{2,1,0:T(8,128)(2,1)S(1)} %all_to_all.63), channel_id=1, replica_groups=mesh['seq'=16,'head'=2] {'head'}, dimensions={0} | all-to-all | bytes 2097152 | tf_op jit(solution)/shard_map/all_to_all | solution.py:181
  (279 shorter events, 147.1 us)
Async XLA Ops:
  8.2 10.7 %all-to-all-start.1 = ((bf16[128,2,512]{2,0,1:T(8,128)(2,1)}), bf16[128,2,512]{2,0,1:T(8,128)(2,1)S(1)}, u32[]{:S(2)}, u32[]{:S(2)}) async-start(bf16[128,2,512]{2,0,1:T(8,128)(2,1)} %bitcast.490), calls=%async_computation.1 | async-start | bytes 524288 | tf_op jit(solution)/shard_map/all_to_all | solution.py:122
  18.9 8.0 %all-to-all-start.2 = ((bf16[128,2,512]{2,0,1:T(8,128)(2,1)}), bf16[128,2,512]{2,0,1:T(8,128)(2,1)S(1)}, u32[]{:S(2)}, u32[]{:S(2)}) async-start(bf16[128,2,512]{2,0,1:T(8,128)(2,1)} %bitcast.489), calls=%async_computation.2 | async-start | bytes 524288 | tf_op jit(solution)/shard_map/all_to_all | solution.py:123
  26.9 15.7 %all-to-all-start = ((bf16[128,2,2048]{2,0,1:T(8,128)(2,1)}), bf16[128,2,2048]{2,0,1:T(8,128)(2,1)S(1)}, u32[]{:S(2)}, u32[]{:S(2)}) async-start(bf16[128,2,2048]{2,0,1:T(8,128)(2,1)} %bitcast.488), calls=%async_computation | async-start | bytes 2097152 | tf_op jit(solution)/shard_map/all_to_all | solution.py:121
  36.5 19.2 %copy-start.14 = (s32[4,128]{1,0:T(4,128)S(1)}, s32[4,128]{1,0:T(4,128)}, u32[]{:S(2)}) copy-start(s32[4,128]{1,0:T(4,128)} %param.16) | copy-start | bytes 6148
  42.6 241.3 %all-to-all-start.3 = ((bf16[16,256,4,256]{3,1,2,0:T(8,128)(2,1)}), bf16[16,256,4,256]{3,1,2,0:T(8,128)(2,1)}, u32[]{:S(2)}, u32[]{:S(2)}) async-start(bf16[16,256,4,256]{3,1,2,0:T(8,128)(2,1)} %broadcast_select_fusion), calls=%async_computation.3 | async-start | bytes 16777216 | tf_op jit(solution)/shard_map/all_to_all | solution.py:150
  50.9 248.9 %all-gather.3.cloned.1.call-start = ((), (), s32[]{:S(2)}) async-start(), calls=%async_computation.5 | async-start | bytes 8912896 | tf_op jit(solution)/shard_map/all_gather | solution.py:12
  305.3 0.6 copy-start.16
  314.6 4.9 copy-start.4
  319.5 9.1 %copy-start.11 = (bf16[2,2,64,256]{3,2,1,0:T(8,128)(2,1)S(1)}, bf16[2,2,64,256]{3,2,1,0:T(8,128)(2,1)}, u32[]{:S(2)}) copy-start(bf16[2,2,64,256]{3,2,1,0:T(8,128)(2,1)} %get-tuple-element.1995) | copy-start | bytes 393220 | tf_op jit(solution)/shard_map/while
  336.2 4.3 copy-start
  352.8 6.0 copy-start.17
  358.8 0.6 copy-start.16
  368.2 4.9 copy-start.4
  373.0 9.1 %copy-start.11 = (bf16[2,2,64,256]{3,2,1,0:T(8,128)(2,1)S(1)}, bf16[2,2,64,256]{3,2,1,0:T(8,128)(2,1)}, u32[]{:S(2)}) copy-start(bf16[2,2,64,256]{3,2,1,0:T(8,128)(2,1)} %get-tuple-element.1995) | copy-start | bytes 393220 | tf_op jit(solution)/shard_map/while
  389.7 4.3 copy-start
  406.3 6.0 copy-start.17
  421.4 4.9 copy-start.5
  443.0 4.3 copy-start.1
  472.6 4.9 copy-start.5
  494.2 4.3 copy-start.1
  516.8 108.1 %copy-start.8 = (bf16[2,2,64,4,128]{4,3,2,1,0:T(4,128)(2,1)S(1)}, bf16[2,2,64,4,128]{4,3,2,1,0:T(4,128)(2,1)}, u32[]{:S(2)}) copy-start(bf16[2,2,64,4,128]{4,3,2,1,0:T(4,128)(2,1)} %get-tuple-element.1807) | copy-start | bytes 786436
  516.8 108.1 %copy-start.9 = (bf16[256,1,256]{2,0,1:T(8,128)(2,1)S(1)}, bf16[256,1,256]{2,0,1:T(8,128)(2,1)}, u32[]{:S(2)}) copy-start(bf16[256,1,256]{2,0,1:T(8,128)(2,1)} %get-tuple-element.1294) | copy-start | bytes 393220
  516.8 108.1 %copy-start.12 = (bf16[128,256]{1,0:T(8,128)(2,1)S(1)}, bf16[128,256]{1,0:T(8,128)(2,1)}, u32[]{:S(2)}) copy-start(bf16[128,256]{1,0:T(8,128)(2,1)} %get-tuple-element.1820) | copy-start | bytes 196612
  516.8 108.1 %copy-start.15 = (s32[1,4,40]{2,1,0:T(4,128)S(1)}, s32[1,4,40]{2,1,0:T(4,128)}, u32[]{:S(2)}) copy-start(s32[1,4,40]{2,1,0:T(4,128)} %get-tuple-element.1302) | copy-start | bytes 1924
  527.2 4.9 copy-start.6
  532.1 9.1 %copy-start.10 = (bf16[2,2,64,256]{3,2,1,0:T(8,128)(2,1)S(1)}, bf16[2,2,64,256]{3,2,1,0:T(8,128)(2,1)}, u32[]{:S(2)}) copy-start(bf16[2,2,64,256]{3,2,1,0:T(8,128)(2,1)} %get-tuple-element.1893) | copy-start | bytes 393220 | tf_op jit(solution)/shard_map/while
  548.8 4.3 copy-start.2
  565.4 4.3 copy-start.13
  580.7 4.9 copy-start.6
  585.6 9.1 %copy-start.10 = (bf16[2,2,64,256]{3,2,1,0:T(8,128)(2,1)S(1)}, bf16[2,2,64,256]{3,2,1,0:T(8,128)(2,1)}, u32[]{:S(2)}) copy-start(bf16[2,2,64,256]{3,2,1,0:T(8,128)(2,1)} %get-tuple-element.1893) | copy-start | bytes 393220 | tf_op jit(solution)/shard_map/while
  602.3 4.3 copy-start.2
  618.9 4.3 copy-start.13
  632.9 4.9 copy-start.7
  654.5 4.3 copy-start.3
  684.2 4.9 copy-start.7
  705.7 4.3 copy-start.3
Sparse Core Ops, SparseCore 0:
  53.9 187.5 all-gather.2
